TPU v7x, 256 devices: a whole 4x4x8 slice. The times are simulated.
256 devices in a mesh: ctx: 32 (over z_hi, x, core), tp: 8 (over y, z_lo).
Axes of the slice: x: 4, y: 4, z: 8 (z_hi: 4, z_lo: 2; z = z_hi * 2 + z_lo), core: 2. Of those that a mesh axis runs over, the one named last changes fastest.
Arguments:
- features: bfloat16 [16384, 3, 4096], P('ctx', None, 'tp'), may hold values from -6 to 6
- short_filter: float32 [3, 7, 4096], P(None, None, 'tp'), may hold values from -2 to 2
- decay_rate: float32 [16, 4096], P(None, 'tp'), may hold values from 0 to 1, as said below
- residue: float32 [16, 4096], P(None, 'tp'), may hold values from -2 to 2
- skip_gain: float32 [4096], P('tp'), may hold values from -4 to 4
- norm_gain: float32 [4096], replicated, may hold values from 0.1 to 1.9
- qkv_weight: bfloat16 [4096, 3, 2048], P('ctx', None, 'tp'), may hold values from -2 to 2
Outputs:
- mixer: bfloat16 [16384, 4096], P('ctx', 'tp')
- attended: bfloat16 [16384, 2048], P('ctx', 'tp')
Inputs may be any that keep to these rules, and one draw needn't show every extreme that they name: `decay_rate`: decay rates are positive.
All inputs are finite; a program needn't handle non-finite values.
Results may differ from a plain program's by a relative error of at most 0.01.
Values may be sent and summed in bfloat16 or wider, within the bound.
No kernel may reach another device: no remote copies, remote signals or barrier semaphores. Data moves between devices by JAX's collectives and lax.ppermute only.
A program may use at most 128 MiB of HBM per device.

v0:
```python
from functools import reduce
import math
import jax
import jax.numpy as jnp
from jax import lax
from jax.sharding import PartitionSpec as P

HD = 128
TAPS = 7
WINDOW = 3
EPSILON = 1e-06
PRECISE = lax.Precision.HIGHEST


def from_behind(value, axis, steps):
    count = lax.axis_size(axis)
    leading, last = (max(0, -steps), min(count, count - steps))
    return lax.ppermute(value, axis, [(source, source + steps) for source in range(leading, last)])


def modal_toeplitz(mixing, decay, block_len):
    distance = jnp.arange(block_len)[:, None] - jnp.arange(block_len)[None, :]
    lag_float = jnp.maximum(distance, 0).astype(jnp.float32)
    channels = mixing.shape[1]
    start = jnp.zeros((channels, block_len, block_len), jnp.float32)

    def add_mode(mode, running):
        weight_row = lax.dynamic_index_in_dim(mixing, mode, 0, keepdims=False)
        rate_row = lax.dynamic_index_in_dim(decay, mode, 0, keepdims=False)
        term = weight_row[:, None, None] * jnp.exp(-rate_row[:, None, None] * lag_float[None])
        return running + term

    summed = lax.fori_loop(0, mixing.shape[0], add_mode, start)
    return jnp.where(distance[None] >= 0, summed, 0.0)


def channel_conv(signal, decay, residue, skip_gain):
    channels, length = signal.shape
    block_len = math.gcd(length, 256)
    block_count = length // block_len
    blocked = signal.reshape(channels, block_count, block_len)
    rate_cols = decay.T
    mode_weights = residue * jnp.sqrt(decay)
    mixing = mode_weights.T
    offsets = jnp.arange(block_len).astype(jnp.float32)
    trailing = jnp.exp(-rate_cols[:, :, None] * (block_len - 1.0 - offsets)[None, None, :])
    block_ends = jnp.einsum("cbs,cns->cnb", blocked, trailing, precision=PRECISE)
    block_ids = jnp.arange(block_count)
    spacing = block_ids[:, None] - 1 - block_ids[None, :]
    powers = (block_len * jnp.maximum(spacing, 0)).astype(jnp.float32)
    carry = jnp.where(
        spacing[None, None] >= 0, jnp.exp(-rate_cols[:, :, None, None] * powers[None, None]), 0.0
    )
    entering = jnp.einsum("cnkb,cnb->cnk", carry, block_ends, precision=PRECISE)
    leading = jnp.exp(-rate_cols[:, :, None] * (offsets + 1.0)[None, None, :])
    across = jnp.einsum("cnk,cns->cks", entering * mixing[:, :, None], leading, precision=PRECISE)
    toeplitz = modal_toeplitz(mode_weights, decay, block_len)
    within = jnp.einsum("cts,cbs->cbt", toeplitz, blocked, precision=PRECISE)
    return (within + across + skip_gain[:, None, None] * blocked).reshape(channels, length)


def on_device(features, short_filter, decay_rate, residue, skip_gain, norm_gain, qkv_weight):
    tok_dev, _, channels = features.shape
    rim_rows = features[tok_dev - (TAPS - 1) :]
    before = from_behind(rim_rows, "ctx", 1)
    extended = jnp.concatenate([before, features], axis=0).astype(jnp.float32)
    short_conv = jnp.zeros((tok_dev, 3, channels), jnp.float32)
    for offset in range(TAPS):
        first_row = TAPS - 1 - offset
        short_conv = (
            short_conv
            + short_filter[:, offset, :][None] * extended[first_row : first_row + tok_dev]
        )
    gated = (short_conv[:, 1] * short_conv[:, 2]).astype(jnp.bfloat16)
    per_device = channels // lax.axis_size("ctx")
    by_channel = lax.all_to_all(gated.T, "ctx", split_axis=0, concat_axis=1, tiled=True)
    first_channel = lax.axis_index("ctx") * per_device
    decay_part = lax.dynamic_slice_in_dim(decay_rate, first_channel, per_device, 1)
    residue_part = lax.dynamic_slice_in_dim(residue, first_channel, per_device, 1)
    skip_part = lax.dynamic_slice_in_dim(skip_gain, first_channel, per_device, 0)
    filtered = channel_conv(
        by_channel.astype(jnp.float32), decay_part, residue_part, skip_part
    ).astype(jnp.bfloat16)
    long_part = lax.all_to_all(filtered, "ctx", split_axis=1, concat_axis=0, tiled=True).T
    mixer = (short_conv[:, 0] * long_part.astype(jnp.float32)).astype(jnp.bfloat16)
    gathered = lax.all_gather(mixer, "tp", axis=1, tiled=True)
    as_float = gathered.astype(jnp.float32)
    inverse = lax.rsqrt(jnp.mean(as_float * as_float, axis=1, keepdims=True) + EPSILON)
    normed = (as_float * inverse * norm_gain[None]).astype(jnp.bfloat16)
    head_cols = qkv_weight.shape[2]
    shard_rows = lax.all_gather(qkv_weight, "ctx", axis=0, tiled=True)
    flat_rows = shard_rows.reshape(shard_rows.shape[0], 3 * head_cols)
    projected = jnp.dot(normed, flat_rows, preferred_element_type=jnp.float32).astype(jnp.bfloat16)
    heads = head_cols // HD
    query = projected[:, :head_cols].reshape(tok_dev, heads, HD)
    kv_pair = projected[:, head_cols:]
    blocks_kv = [kv_pair]
    for lag_step in range(WINDOW - 1):
        blocks_kv.append(from_behind(blocks_kv[-1], "ctx", 1))
    position = lax.axis_index("ctx")
    row_ids = jnp.arange(tok_dev)
    causal = row_ids[:, None] >= row_ids[None, :]
    score_list = []
    for lag_step in range(WINDOW):
        keys = blocks_kv[lag_step][:, :head_cols].reshape(tok_dev, heads, HD)
        scores = jnp.einsum(
            "thd,shd->hts", query, keys, preferred_element_type=jnp.float32
        ) / math.sqrt(HD)
        if lag_step == 0:
            allowed = causal
        else:
            allowed = jnp.broadcast_to(position >= lag_step, causal.shape)
        score_list.append(jnp.where(allowed[None], scores, -jnp.inf))
    peak = reduce(jnp.maximum, [jnp.max(entry, axis=2) for entry in score_list])
    total = jnp.zeros((heads, tok_dev), jnp.float32)
    output = jnp.zeros((tok_dev, heads, HD), jnp.float32)
    for lag_step in range(WINDOW):
        expo = jnp.exp(score_list[lag_step] - peak[:, :, None])
        total = total + jnp.sum(expo, axis=2)
        values = blocks_kv[lag_step][:, head_cols:].reshape(tok_dev, heads, HD)
        output = output + jnp.einsum(
            "hts,shd->thd", expo.astype(jnp.bfloat16), values, preferred_element_type=jnp.float32
        )
    attended = (output / total.T[:, :, None]).astype(jnp.bfloat16).reshape(tok_dev, head_cols)
    return (mixer, attended)


def solution(mesh):
    placed = (
        P("ctx", None, "tp"),
        P(None, None, "tp"),
        P(None, "tp"),
        P(None, "tp"),
        P("tp"),
        P(),
        P("ctx", None, "tp"),
    )
    return jax.shard_map(
        on_device,
        mesh=mesh,
        in_specs=placed,
        out_specs=(P("ctx", "tp"), P("ctx", "tp")),
        check_vma=False,
    )
```

profile of v0, /device:TPU:128, one launch (start us, length us, event | category | flops | bytes accessed | tf_op | source)
XLA Modules:
  0.0 409.7 jit_solution(15432068327113039703)
XLA Ops:
  13.4 79.2 %while.14 = (s32[]{:T(128)}, f32[16,256,256]{2,1,0:T(8,128)}, f32[16,16]{1,0:T(8,128)S(1)}, f32[16,16]{1,0:T(8,128)S(1)}, s32[]{:T(128)}, /*index=5*/s32[]{:T(128)}) while((s32[]{:T(128)}, f32[16,256,256]{2,1,0:T(8,128)}, f32[16,16]{1,0:T(8,128)S(1)}, f32[16,16]{1,0:T(8,128)S(1)}, s32[]{:T(128)}, /*index=5*/s32[]{:T(128)}) %tuple.60), condition=%wide.region_1.2_spmd.clone, body=%wide.region_0.1_spmd.clone.sunk | while | flops 4390931 | bytes 8913363 | solution.py:33
  16.4 5.0 %select_add_fusion.2 = f32[16,256,256]{2,1,0:T(8,128)} fusion(f32[16,256,256]{2,1,0:T(8,128)} %get-tuple-element.195, f32[256,256]{1,0:T(8,128)S(1)} %maximum_convert_fusion.3, f32[16]{0:T(128)S(1)} %get-tuple-element.186, f32[16]{0:T(128)S(1)} %get-tuple-element.187, pred[]{:T(512)S(6)} %compare.3), kind=kLoop, calls=%fused_computation.1.clone.1 | loop fusion | flops 4194304 | bytes 8650881 | tf_op jit(solution)/shard_map/while/body/eval_jaxpr/add | solution.py:31
  21.5 5.0 %select_add_fusion.2 = f32[16,256,256]{2,1,0:T(8,128)} fusion(f32[16,256,256]{2,1,0:T(8,128)} %get-tuple-element.195, f32[256,256]{1,0:T(8,128)S(1)} %maximum_convert_fusion.3, f32[16]{0:T(128)S(1)} %get-tuple-element.186, f32[16]{0:T(128)S(1)} %get-tuple-element.187, pred[]{:T(512)S(6)} %compare.3), kind=kLoop, calls=%fused_computation.1.clone.1 | loop fusion | flops 4194304 | bytes 8650881 | tf_op jit(solution)/shard_map/while/body/eval_jaxpr/add | solution.py:31
  26.5 5.0 %select_add_fusion.2 = f32[16,256,256]{2,1,0:T(8,128)} fusion(f32[16,256,256]{2,1,0:T(8,128)} %get-tuple-element.195, f32[256,256]{1,0:T(8,128)S(1)} %maximum_convert_fusion.3, f32[16]{0:T(128)S(1)} %get-tuple-element.186, f32[16]{0:T(128)S(1)} %get-tuple-element.187, pred[]{:T(512)S(6)} %compare.3), kind=kLoop, calls=%fused_computation.1.clone.1 | loop fusion | flops 4194304 | bytes 8650881 | tf_op jit(solution)/shard_map/while/body/eval_jaxpr/add | solution.py:31
  31.6 5.0 %select_add_fusion.2 = f32[16,256,256]{2,1,0:T(8,128)} fusion(f32[16,256,256]{2,1,0:T(8,128)} %get-tuple-element.195, f32[256,256]{1,0:T(8,128)S(1)} %maximum_convert_fusion.3, f32[16]{0:T(128)S(1)} %get-tuple-element.186, f32[16]{0:T(128)S(1)} %get-tuple-element.187, pred[]{:T(512)S(6)} %compare.3), kind=kLoop, calls=%fused_computation.1.clone.1 | loop fusion | flops 4194304 | bytes 8650881 | tf_op jit(solution)/shard_map/while/body/eval_jaxpr/add | solution.py:31
  36.7 5.0 %select_add_fusion.2 = f32[16,256,256]{2,1,0:T(8,128)} fusion(f32[16,256,256]{2,1,0:T(8,128)} %get-tuple-element.195, f32[256,256]{1,0:T(8,128)S(1)} %maximum_convert_fusion.3, f32[16]{0:T(128)S(1)} %get-tuple-element.186, f32[16]{0:T(128)S(1)} %get-tuple-element.187, pred[]{:T(512)S(6)} %compare.3), kind=kLoop, calls=%fused_computation.1.clone.1 | loop fusion | flops 4194304 | bytes 8650881 | tf_op jit(solution)/shard_map/while/body/eval_jaxpr/add | solution.py:31
  41.8 5.0 %select_add_fusion.2 = f32[16,256,256]{2,1,0:T(8,128)} fusion(f32[16,256,256]{2,1,0:T(8,128)} %get-tuple-element.195, f32[256,256]{1,0:T(8,128)S(1)} %maximum_convert_fusion.3, f32[16]{0:T(128)S(1)} %get-tuple-element.186, f32[16]{0:T(128)S(1)} %get-tuple-element.187, pred[]{:T(512)S(6)} %compare.3), kind=kLoop, calls=%fused_computation.1.clone.1 | loop fusion | flops 4194304 | bytes 8650881 | tf_op jit(solution)/shard_map/while/body/eval_jaxpr/add | solution.py:31
  46.9 5.0 %select_add_fusion.2 = f32[16,256,256]{2,1,0:T(8,128)} fusion(f32[16,256,256]{2,1,0:T(8,128)} %get-tuple-element.195, f32[256,256]{1,0:T(8,128)S(1)} %maximum_convert_fusion.3, f32[16]{0:T(128)S(1)} %get-tuple-element.186, f32[16]{0:T(128)S(1)} %get-tuple-element.187, pred[]{:T(512)S(6)} %compare.3), kind=kLoop, calls=%fused_computation.1.clone.1 | loop fusion | flops 4194304 | bytes 8650881 | tf_op jit(solution)/shard_map/while/body/eval_jaxpr/add | solution.py:31
  52.0 5.0 %select_add_fusion.2 = f32[16,256,256]{2,1,0:T(8,128)} fusion(f32[16,256,256]{2,1,0:T(8,128)} %get-tuple-element.195, f32[256,256]{1,0:T(8,128)S(1)} %maximum_convert_fusion.3, f32[16]{0:T(128)S(1)} %get-tuple-element.186, f32[16]{0:T(128)S(1)} %get-tuple-element.187, pred[]{:T(512)S(6)} %compare.3), kind=kLoop, calls=%fused_computation.1.clone.1 | loop fusion | flops 4194304 | bytes 8650881 | tf_op jit(solution)/shard_map/while/body/eval_jaxpr/add | solution.py:31
  57.0 5.0 %select_add_fusion.2 = f32[16,256,256]{2,1,0:T(8,128)} fusion(f32[16,256,256]{2,1,0:T(8,128)} %get-tuple-element.195, f32[256,256]{1,0:T(8,128)S(1)} %maximum_convert_fusion.3, f32[16]{0:T(128)S(1)} %get-tuple-element.186, f32[16]{0:T(128)S(1)} %get-tuple-element.187, pred[]{:T(512)S(6)} %compare.3), kind=kLoop, calls=%fused_computation.1.clone.1 | loop fusion | flops 4194304 | bytes 8650881 | tf_op jit(solution)/shard_map/while/body/eval_jaxpr/add | solution.py:31
  62.1 5.0 %select_add_fusion.2 = f32[16,256,256]{2,1,0:T(8,128)} fusion(f32[16,256,256]{2,1,0:T(8,128)} %get-tuple-element.195, f32[256,256]{1,0:T(8,128)S(1)} %maximum_convert_fusion.3, f32[16]{0:T(128)S(1)} %get-tuple-element.186, f32[16]{0:T(128)S(1)} %get-tuple-element.187, pred[]{:T(512)S(6)} %compare.3), kind=kLoop, calls=%fused_computation.1.clone.1 | loop fusion | flops 4194304 | bytes 8650881 | tf_op jit(solution)/shard_map/while/body/eval_jaxpr/add | solution.py:31
  67.2 5.0 %select_add_fusion.2 = f32[16,256,256]{2,1,0:T(8,128)} fusion(f32[16,256,256]{2,1,0:T(8,128)} %get-tuple-element.195, f32[256,256]{1,0:T(8,128)S(1)} %maximum_convert_fusion.3, f32[16]{0:T(128)S(1)} %get-tuple-element.186, f32[16]{0:T(128)S(1)} %get-tuple-element.187, pred[]{:T(512)S(6)} %compare.3), kind=kLoop, calls=%fused_computation.1.clone.1 | loop fusion | flops 4194304 | bytes 8650881 | tf_op jit(solution)/shard_map/while/body/eval_jaxpr/add | solution.py:31
  72.3 5.0 %select_add_fusion.2 = f32[16,256,256]{2,1,0:T(8,128)} fusion(f32[16,256,256]{2,1,0:T(8,128)} %get-tuple-element.195, f32[256,256]{1,0:T(8,128)S(1)} %maximum_convert_fusion.3, f32[16]{0:T(128)S(1)} %get-tuple-element.186, f32[16]{0:T(128)S(1)} %get-tuple-element.187, pred[]{:T(512)S(6)} %compare.3), kind=kLoop, calls=%fused_computation.1.clone.1 | loop fusion | flops 4194304 | bytes 8650881 | tf_op jit(solution)/shard_map/while/body/eval_jaxpr/add | solution.py:31
  87.5 5.0 %select_add_fusion.2 = f32[16,256,256]{2,1,0:T(8,128)} fusion(f32[16,256,256]{2,1,0:T(8,128)} %get-tuple-element.195, f32[256,256]{1,0:T(8,128)S(1)} %maximum_convert_fusion.3, f32[16]{0:T(128)S(1)} %get-tuple-element.186, f32[16]{0:T(128)S(1)} %get-tuple-element.187, pred[]{:T(512)S(6)} %compare.3), kind=kLoop, calls=%fused_computation.1.clone.1 | loop fusion | flops 4194304 | bytes 8650881 | tf_op jit(solution)/shard_map/while/body/eval_jaxpr/add | solution.py:31
  96.8 7.0 %fusion.19 = f32[512,3,512]{0,2,1:T(8,128)S(1)} fusion(f32[518,3,512]{0,2,1:T(8,128)S(1)} %maximum_convert_fusion.1, f32[3,512]{1,0:T(4,128)S(1)} %copy-done.6, f32[3,512]{1,0:T(4,128)S(1)} %copy-done.7, f32[3,512]{1,0:T(4,128)S(1)} %copy-done.8, f32[3,512]{1,0:T(4,128)S(1)} %copy-done.9, f32[3,512]{1,0:T(4,128)S(1)} %copy-done.10, ...), kind=kLoop, calls=%fused_computation.24 | loop fusion | flops 10223616 | bytes 25208832 | tf_op jit(solution)/shard_map/add | solution.py:71
  104.8 10.8 %all-to-all-start = ((bf16[32,16,512]{2,1,0:T(8,128)(2,1)}), bf16[32,16,512]{2,1,0:T(8,128)(2,1)}, u32[]{:S(2)}, u32[]{:S(2)}) async-start(bf16[32,16,512]{2,1,0:T(8,128)(2,1)} %bitcast.103), calls=%async_computation | async-start | bytes 1048576 | tf_op jit(solution)/shard_map/all_to_all | solution.py:76
  117.0 13.6 %all-to-all-done = bf16[32,16,512]{2,1,0:T(8,128)(2,1)} async-done(((bf16[32,16,512]{2,1,0:T(8,128)(2,1)}), bf16[32,16,512]{2,1,0:T(8,128)(2,1)}, u32[]{:S(2)}, u32[]{:S(2)}) %all-to-all-start) | async-done | bytes 524320 | tf_op jit(solution)/shard_map/all_to_all | solution.py:76
  136.3 14.1 %fusion.5 = f32[16,16,1,64]{3,2,1,0:T(1,128)S(1)} fusion(f32[16,16,64,1]{2,3,1,0:T(1,128)S(1)} %bitcast.108, f32[64,64]{1,0:T(8,128)S(1)} %multiply_convert_fusion, f32[16,16]{1,0:T(8,128)S(1)} %copy.30, pred[64,64]{1,0:T(8,128)(4,1)S(1)} %fusion.97), kind=kOutput, calls=%fused_computation.10 | convolution fusion | flops 14680064 | bytes 152576 | tf_op jit(solution)/shard_map/cnkb,cnb->cnk/dot_general | solution.py:54
  158.4 21.9 %all_to_all.26 = bf16[16,32,512]{2,0,1:T(8,128)(2,1)S(1)} all-to-all(bf16[16,32,512]{2,0,1:T(8,128)(2,1)S(1)} %copy.33), channel_id=1, replica_groups=mesh['ctx'=32,'tp'=8] {'ctx'}, dimensions={1} | all-to-all | bytes 1048576 | tf_op jit(solution)/shard_map/all_to_all | solution.py:84
  184.3 89.4 %all-gather.3.cloned.1.call-done = bf16[512,4096]{0,1:T(8,128)(2,1)} async-done(((bf16[512,512]{0,1:T(8,128)(2,1)}), bf16[512,4096]{0,1:T(8,128)(2,1)}) %all-gather.3.cloned.1.call-update) | async-done | bytes 4194320 | tf_op jit(solution)/shard_map/all_gather | solution.py:86
  276.9 71.4 %all-gather.5.cloned.1.call-done = bf16[4096,3,256]{0,2,1:T(8,128)(2,1)} async-done(((bf16[128,3,256]{0,2,1:T(8,128)(2,1)}), bf16[4096,3,256]{0,2,1:T(8,128)(2,1)}) %all-gather.5.cloned.1.call-update) | async-done | bytes 6291472 | tf_op jit(solution)/shard_map/all_gather | solution.py:91
  348.3 8.2 %fusion.36 = bf16[512,768]{1,0:T(8,128)(2,1)S(1)} fusion(bf16[4096,768]{0,1:T(8,128)(2,1)} %bitcast.112, bf16[512,4096]{0,1:T(8,128)(2,1)} %all-gather.3.cloned.1.call-done, f32[4096]{0:T(1024)S(1)} %copy-done.12, f32[512]{0:T(512)S(1)} %add_rsqrt_fusion), kind=kOutput, calls=%fused_computation.54 | convolution fusion | flops 3230007296 | bytes 11290624 | tf_op jit(solution)/shard_map/dot_general | solution.py:93
  361.5 11.9 %collective-permute-done.1 = bf16[512,512]{1,0:T(8,128)(2,1)} collective-permute-done((bf16[512,512]{1,0:T(8,128)(2,1)S(1)}, bf16[512,512]{1,0:T(8,128)(2,1)}, u32[]{:S(2)}, u32[]{:S(2)}) %collective-permute-start.1) | collective-permute-done | bytes 524320 | tf_op jit(solution)/shard_map/ppermute | solution.py:18
  377.3 16.9 %collective-permute-done.2 = bf16[512,512]{1,0:T(8,128)(2,1)} collective-permute-done((bf16[512,512]{1,0:T(8,128)(2,1)}, bf16[512,512]{1,0:T(8,128)(2,1)}, u32[]{:S(2)}, u32[]{:S(2)}) %collective-permute-start.2) | collective-permute-done | bytes 524320 | tf_op jit(solution)/shard_map/ppermute | solution.py:18
  (121 shorter events, 64.4 us)
Async XLA Ops:
  8.9 87.0 %collective-permute-start = (bf16[6,3,512]{0,2,1:T(8,128)(2,1)}, bf16[6,3,512]{0,2,1:T(8,128)(2,1)S(1)}, u32[]{:S(2)}, u32[]{:S(2)}) collective-permute-start(bf16[6,3,512]{0,2,1:T(8,128)(2,1)} %copy.27), channel_id=1, source_target_pairs={{0,8},{8,16},{16,24},{24,32},{32,40},{40,48},{48,56},{56,64},{64,7... | collective-permute-start | bytes 55304 | tf_op jit(solution)/shard_map/ppermute | solution.py:18
  13.4 81.0 %copy-start.3 = (bf16[512,3,512]{2,0,1:T(8,128)(2,1)S(1)}, bf16[512,3,512]{2,0,1:T(8,128)(2,1)}, u32[]{:S(2)}) copy-start(bf16[512,3,512]{2,0,1:T(8,128)(2,1)} %param.9) | copy-start | bytes 4718596
  95.1 1.7 copy-start.6
  95.1 1.7 copy-start.7
  95.1 1.7 copy-start.8
  95.1 1.7 copy-start.9
  95.2 1.7 copy-start.10
  95.2 1.7 copy-start.11
  104.8 25.7 %all-to-all-start = ((bf16[32,16,512]{2,1,0:T(8,128)(2,1)}), bf16[32,16,512]{2,1,0:T(8,128)(2,1)}, u32[]{:S(2)}, u32[]{:S(2)}) async-start(bf16[32,16,512]{2,1,0:T(8,128)(2,1)} %bitcast.103), calls=%async_computation | async-start | bytes 1048576 | tf_op jit(solution)/shard_map/all_to_all | solution.py:76
  115.6 158.1 %all-gather.3.cloned.1.call-start = ((), (), s32[]{:S(2)}) async-start(), calls=%async_computation.2 | async-start | bytes 4718592 | tf_op jit(solution)/shard_map/all_gather | solution.py:86
  136.3 15.4 %copy-start = (f32[16,256,256]{2,1,0:T(8,128)S(1)}, f32[16,256,256]{2,1,0:T(8,128)}, u32[]{:S(2)}) copy-start(f32[16,256,256]{2,1,0:T(8,128)} %get-tuple-element.96) | copy-start | bytes 12582916
  136.3 15.4 %copy-start.1 = (bf16[16,64,256]{2,1,0:T(8,128)(2,1)S(1)}, bf16[16,64,256]{2,1,0:T(8,128)(2,1)}, u32[]{:S(2)}) copy-start(bf16[16,64,256]{2,1,0:T(8,128)(2,1)} %reshape.174) | copy-start | bytes 1572868
  155.0 26.3 %copy-start.5 = (bf16[128,3,256]{2,0,1:T(8,128)(2,1)S(1)}, bf16[128,3,256]{2,0,1:T(8,128)(2,1)}, u32[]{:S(2)}) copy-start(bf16[128,3,256]{2,0,1:T(8,128)(2,1)} %param.15) | copy-start | bytes 589828
  181.3 167.0 %copy-start.12 = (f32[4096]{0:T(1024)S(1)}, f32[4096]{0:T(1024)}, u32[]{:S(2)}) copy-start(f32[4096]{0:T(1024)} %param.14) | copy-start | bytes 49156
  181.3 167.0 %all-gather.5.cloned.1.call-start = ((), (), s32[]{:S(2)}) async-start(), calls=%async_computation.3 | async-start | bytes 6488064 | tf_op jit(solution)/shard_map/all_gather | solution.py:91
  356.5 16.9 %collective-permute-start.1 = (bf16[512,512]{1,0:T(8,128)(2,1)S(1)}, bf16[512,512]{1,0:T(8,128)(2,1)}, u32[]{:S(2)}, u32[]{:S(2)}) collective-permute-start(bf16[512,512]{1,0:T(8,128)(2,1)S(1)} %slice.119), channel_id=1, source_target_pairs={{0,8},{8,16},{16,24},{24,32},{32,40},{40,48},{48,56},{56,64},{64,7... | collective-permute-start | bytes 1572872 | tf_op jit(solution)/shard_map/ppermute | solution.py:18
  373.4 20.7 %collective-permute-start.2 = (bf16[512,512]{1,0:T(8,128)(2,1)}, bf16[512,512]{1,0:T(8,128)(2,1)}, u32[]{:S(2)}, u32[]{:S(2)}) collective-permute-start(bf16[512,512]{1,0:T(8,128)(2,1)} %collective-permute-done.1), channel_id=1, source_target_pairs={{0,8},{8,16},{16,24},{24,32},{32,40},{40,48},{48,56},{56,64},{64,7... | collective-permute-start | bytes 1572872 | tf_op jit(solution)/shard_map/ppermute | solution.py:18
  396.1 3.0 copy-start.2
  400.4 1.0 copy-start.4
Sparse Core Ops, SparseCore 0:
  181.4 92.3 all-gather.2
  276.8 71.4 all-gather.4
where the time goes:
time: 411 us; the launch traced here: 410 us
  waiting for transfers between devices  203 us (49%)
  other arithmetic  94.5 us (23%)
  matrix products  34.9 us (8%)
  local copies, waits for them, and re-layouts  23.4 us (6%)
  blocking collectives  21.9 us (5%)
  starting transfers between devices  17.3 us (4%)
  between operations  14.4 us (4%)
    all_gather x1, waiting for transfers between devices, on_device(): gathered = lax.all_gather(mixer, 'tp', axis=1, tiled=True)  89.4 us
    add x16, other arithmetic, add_mode(): return running + term  78.5 us
    all_gather x1, waiting for transfers between devices, on_device(): shard_rows = lax.all_gather(qkv_weight, 'ctx', axis=0, tiled=True)  71.4 us
    ppermute x3, waiting for transfers between devices, from_behind(): lax.ppermute(value, axis, [(source, source + steps) for source in range(l...  28.8 us
    all_to_all x1, blocking collectives, on_device(): lax.all_to_all(filtered, 'ctx', split_axis=1, concat_axis=0, tiled=True)  21.9 us
    dot_general x1, matrix products, channel_conv(): entering = jnp.einsum('cnkb,cnb->cnk', carry, block_ends, precision=PRECISE)  14.1 us
    all_to_all x1, waiting for transfers between devices, on_device(): lax.all_to_all(gated.T, 'ctx', split_axis=0, concat_axis=1, tiled=True)  13.6 us
    all_to_all x1, starting transfers between devices, on_device(): lax.all_to_all(gated.T, 'ctx', split_axis=0, concat_axis=1, tiled=True)  10.8 us
  transfers between devices with their start and end apart: 6, of which 5 were waited for; matrix products, arithmetic and copies ran while one was open for 24% of the time, Pallas kernels for 0%

commit v1 on v0

--- a/solution.py
+++ b/solution.py
@@ -4,12 +4,20 @@
 import jax.numpy as jnp
 from jax import lax
 from jax.sharding import PartitionSpec as P
+from jax.lax import all_to_all, axis_size
 
 HD = 128
 TAPS = 7
 WINDOW = 3
 EPSILON = 1e-06
 PRECISE = lax.Precision.HIGHEST
+
+
+def edit_strips_all(piece_in):
+    o_now = axis_size("tp")
+    shaped = jnp.stack([piece_in] * o_now, axis=0)
+    piece_out = all_to_all(shaped, "tp", 0, 0)
+    return jnp.concatenate(piece_out, axis=1)
 
 
 def from_behind(value, axis, steps):
@@ -83,7 +91,7 @@
     ).astype(jnp.bfloat16)
     long_part = lax.all_to_all(filtered, "ctx", split_axis=1, concat_axis=0, tiled=True).T
     mixer = (short_conv[:, 0] * long_part.astype(jnp.float32)).astype(jnp.bfloat16)
-    gathered = lax.all_gather(mixer, "tp", axis=1, tiled=True)
+    gathered = edit_strips_all(mixer)
     as_float = gathered.astype(jnp.float32)
     inverse = lax.rsqrt(jnp.mean(as_float * as_float, axis=1, keepdims=True) + EPSILON)
     normed = (as_float * inverse * norm_gain[None]).astype(jnp.bfloat16)

time: 411 us -> 310 us (0.75)
  waiting for transfers between devices: 203 us -> 89.8 us
  starting transfers between devices: 17.3 us -> 22.8 us
  other arithmetic: 94.5 us -> 99.4 us
    all_gather x1 -> x0, waiting for transfers between devices: 89.4 us -> none  [on_device(): gathered = lax.all_gather(mixer, 'tp', axis=1, tiled=True)]
    all_gather x1, waiting for transfers between devices: 71.4 us -> 0.01 us  [on_device(): shard_rows = lax.all_gather(qkv_weight, 'ctx', axis=0, tiled=True)]
    all_to_all x0 -> x1, waiting for transfers between devices: none -> 48.8 us  [edit_strips_all(): piece_out = all_to_all(shaped, 'tp', 0, 0)]
    all_to_all x0 -> x1, starting transfers between devices: none -> 5.81 us  [edit_strips_all(): piece_out = all_to_all(shaped, 'tp', 0, 0)]
    convert_element_type x0 -> x1, other arithmetic: none -> 4.18 us  [on_device(): normed = (as_float * inverse * norm_gain[None]).astype(jnp.bfloat16)]
  transfers between devices with their start and end apart: 6 -> 6, of which waited for: 5 -> 4; matrix products, arithmetic and copies ran while one was open for 24% -> 46% of each run, Pallas kernels for 0% -> 0%
where the time goes in v1:
time: 310 us; the launch traced here: 309 us
  other arithmetic  99.4 us (32%)
  waiting for transfers between devices  89.8 us (29%)
  matrix products  34.3 us (11%)
  local copies, waits for them, and re-layouts  26.4 us (9%)
  starting transfers between devices  22.8 us (7%)
  blocking collectives  21.4 us (7%)
  between operations  14.4 us (5%)
    add x16, other arithmetic, add_mode(): return running + term  80 us
    all_to_all x1, waiting for transfers between devices, edit_strips_all(): piece_out = all_to_all(shaped, 'tp', 0, 0)  48.8 us
    ppermute x3, waiting for transfers between devices, from_behind(): lax.ppermute(value, axis, [(source, source + steps) for source in range(l...  27.6 us
    all_to_all x1, blocking collectives, on_device(): lax.all_to_all(filtered, 'ctx', split_axis=1, concat_axis=0, tiled=True)  21.4 us
    dot_general x1, matrix products, channel_conv(): entering = jnp.einsum('cnkb,cnb->cnk', carry, block_ends, precision=PRECISE)  14.1 us
    all_to_all x1, waiting for transfers between devices, on_device(): lax.all_to_all(gated.T, 'ctx', split_axis=0, concat_axis=1, tiled=True)  13.4 us
    all_to_all x1, starting transfers between devices, on_device(): lax.all_to_all(gated.T, 'ctx', split_axis=0, concat_axis=1, tiled=True)  11 us
    unnamed x37, local copies, waits for them, and re-layouts  8.11 us
  transfers between devices with their start and end apart: 6, of which 4 were waited for; matrix products, arithmetic and copies ran while one was open for 46% of the time, Pallas kernels for 0%

profile of v1, /device:TPU:128, one launch (start us, length us, event | category | flops | bytes accessed | tf_op | source)
XLA Modules:
  0.0 308.6 jit_solution(7849500866267992889)
XLA Ops:
  15.2 80.7 %while.14 = (s32[]{:T(128)}, f32[16,256,256]{2,1,0:T(8,128)}, f32[16,16]{1,0:T(8,128)S(1)}, f32[16,16]{1,0:T(8,128)S(1)}, s32[]{:T(128)}, /*index=5*/s32[]{:T(128)}) while((s32[]{:T(128)}, f32[16,256,256]{2,1,0:T(8,128)}, f32[16,16]{1,0:T(8,128)S(1)}, f32[16,16]{1,0:T(8,128)S(1)}, s32[]{:T(128)}, /*index=5*/s32[]{:T(128)}) %tuple.60), condition=%wide.region_1.2_spmd.clone, body=%wide.region_0.1_spmd.clone.sunk | while | flops 4390931 | bytes 8913363 | solution.py:41
  18.3 5.1 %select_add_fusion.2 = f32[16,256,256]{2,1,0:T(8,128)} fusion(f32[16,256,256]{2,1,0:T(8,128)} %get-tuple-element.195, f32[256,256]{1,0:T(8,128)S(1)} %maximum_convert_fusion.3, f32[16]{0:T(128)S(1)} %get-tuple-element.186, f32[16]{0:T(128)S(1)} %get-tuple-element.187, pred[]{:T(512)S(6)} %compare.3), kind=kLoop, calls=%fused_computation.1.clone.1 | loop fusion | flops 4194304 | bytes 8650881 | tf_op jit(solution)/shard_map/while/body/eval_jaxpr/add | solution.py:39
  23.4 5.1 %select_add_fusion.2 = f32[16,256,256]{2,1,0:T(8,128)} fusion(f32[16,256,256]{2,1,0:T(8,128)} %get-tuple-element.195, f32[256,256]{1,0:T(8,128)S(1)} %maximum_convert_fusion.3, f32[16]{0:T(128)S(1)} %get-tuple-element.186, f32[16]{0:T(128)S(1)} %get-tuple-element.187, pred[]{:T(512)S(6)} %compare.3), kind=kLoop, calls=%fused_computation.1.clone.1 | loop fusion | flops 4194304 | bytes 8650881 | tf_op jit(solution)/shard_map/while/body/eval_jaxpr/add | solution.py:39
  28.6 5.1 %select_add_fusion.2 = f32[16,256,256]{2,1,0:T(8,128)} fusion(f32[16,256,256]{2,1,0:T(8,128)} %get-tuple-element.195, f32[256,256]{1,0:T(8,128)S(1)} %maximum_convert_fusion.3, f32[16]{0:T(128)S(1)} %get-tuple-element.186, f32[16]{0:T(128)S(1)} %get-tuple-element.187, pred[]{:T(512)S(6)} %compare.3), kind=kLoop, calls=%fused_computation.1.clone.1 | loop fusion | flops 4194304 | bytes 8650881 | tf_op jit(solution)/shard_map/while/body/eval_jaxpr/add | solution.py:39
  33.7 5.1 %select_add_fusion.2 = f32[16,256,256]{2,1,0:T(8,128)} fusion(f32[16,256,256]{2,1,0:T(8,128)} %get-tuple-element.195, f32[256,256]{1,0:T(8,128)S(1)} %maximum_convert_fusion.3, f32[16]{0:T(128)S(1)} %get-tuple-element.186, f32[16]{0:T(128)S(1)} %get-tuple-element.187, pred[]{:T(512)S(6)} %compare.3), kind=kLoop, calls=%fused_computation.1.clone.1 | loop fusion | flops 4194304 | bytes 8650881 | tf_op jit(solution)/shard_map/while/body/eval_jaxpr/add | solution.py:39
  38.9 5.1 %select_add_fusion.2 = f32[16,256,256]{2,1,0:T(8,128)} fusion(f32[16,256,256]{2,1,0:T(8,128)} %get-tuple-element.195, f32[256,256]{1,0:T(8,128)S(1)} %maximum_convert_fusion.3, f32[16]{0:T(128)S(1)} %get-tuple-element.186, f32[16]{0:T(128)S(1)} %get-tuple-element.187, pred[]{:T(512)S(6)} %compare.3), kind=kLoop, calls=%fused_computation.1.clone.1 | loop fusion | flops 4194304 | bytes 8650881 | tf_op jit(solution)/shard_map/while/body/eval_jaxpr/add | solution.py:39
  44.0 5.1 %select_add_fusion.2 = f32[16,256,256]{2,1,0:T(8,128)} fusion(f32[16,256,256]{2,1,0:T(8,128)} %get-tuple-element.195, f32[256,256]{1,0:T(8,128)S(1)} %maximum_convert_fusion.3, f32[16]{0:T(128)S(1)} %get-tuple-element.186, f32[16]{0:T(128)S(1)} %get-tuple-element.187, pred[]{:T(512)S(6)} %compare.3), kind=kLoop, calls=%fused_computation.1.clone.1 | loop fusion | flops 4194304 | bytes 8650881 | tf_op jit(solution)/shard_map/while/body/eval_jaxpr/add | solution.py:39
  49.2 5.1 %select_add_fusion.2 = f32[16,256,256]{2,1,0:T(8,128)} fusion(f32[16,256,256]{2,1,0:T(8,128)} %get-tuple-element.195, f32[256,256]{1,0:T(8,128)S(1)} %maximum_convert_fusion.3, f32[16]{0:T(128)S(1)} %get-tuple-element.186, f32[16]{0:T(128)S(1)} %get-tuple-element.187, pred[]{:T(512)S(6)} %compare.3), kind=kLoop, calls=%fused_computation.1.clone.1 | loop fusion | flops 4194304 | bytes 8650881 | tf_op jit(solution)/shard_map/while/body/eval_jaxpr/add | solution.py:39
  54.4 5.2 %select_add_fusion.2 = f32[16,256,256]{2,1,0:T(8,128)} fusion(f32[16,256,256]{2,1,0:T(8,128)} %get-tuple-element.195, f32[256,256]{1,0:T(8,128)S(1)} %maximum_convert_fusion.3, f32[16]{0:T(128)S(1)} %get-tuple-element.186, f32[16]{0:T(128)S(1)} %get-tuple-element.187, pred[]{:T(512)S(6)} %compare.3), kind=kLoop, calls=%fused_computation.1.clone.1 | loop fusion | flops 4194304 | bytes 8650881 | tf_op jit(solution)/shard_map/while/body/eval_jaxpr/add | solution.py:39
  59.6 5.1 %select_add_fusion.2 = f32[16,256,256]{2,1,0:T(8,128)} fusion(f32[16,256,256]{2,1,0:T(8,128)} %get-tuple-element.195, f32[256,256]{1,0:T(8,128)S(1)} %maximum_convert_fusion.3, f32[16]{0:T(128)S(1)} %get-tuple-element.186, f32[16]{0:T(128)S(1)} %get-tuple-element.187, pred[]{:T(512)S(6)} %compare.3), kind=kLoop, calls=%fused_computation.1.clone.1 | loop fusion | flops 4194304 | bytes 8650881 | tf_op jit(solution)/shard_map/while/body/eval_jaxpr/add | solution.py:39
  64.8 5.2 %select_add_fusion.2 = f32[16,256,256]{2,1,0:T(8,128)} fusion(f32[16,256,256]{2,1,0:T(8,128)} %get-tuple-element.195, f32[256,256]{1,0:T(8,128)S(1)} %maximum_convert_fusion.3, f32[16]{0:T(128)S(1)} %get-tuple-element.186, f32[16]{0:T(128)S(1)} %get-tuple-element.187, pred[]{:T(512)S(6)} %compare.3), kind=kLoop, calls=%fused_computation.1.clone.1 | loop fusion | flops 4194304 | bytes 8650881 | tf_op jit(solution)/shard_map/while/body/eval_jaxpr/add | solution.py:39
  70.1 5.1 %select_add_fusion.2 = f32[16,256,256]{2,1,0:T(8,128)} fusion(f32[16,256,256]{2,1,0:T(8,128)} %get-tuple-element.195, f32[256,256]{1,0:T(8,128)S(1)} %maximum_convert_fusion.3, f32[16]{0:T(128)S(1)} %get-tuple-element.186, f32[16]{0:T(128)S(1)} %get-tuple-element.187, pred[]{:T(512)S(6)} %compare.3), kind=kLoop, calls=%fused_computation.1.clone.1 | loop fusion | flops 4194304 | bytes 8650881 | tf_op jit(solution)/shard_map/while/body/eval_jaxpr/add | solution.py:39
  75.2 5.2 %select_add_fusion.2 = f32[16,256,256]{2,1,0:T(8,128)} fusion(f32[16,256,256]{2,1,0:T(8,128)} %get-tuple-element.195, f32[256,256]{1,0:T(8,128)S(1)} %maximum_convert_fusion.3, f32[16]{0:T(128)S(1)} %get-tuple-element.186, f32[16]{0:T(128)S(1)} %get-tuple-element.187, pred[]{:T(512)S(6)} %compare.3), kind=kLoop, calls=%fused_computation.1.clone.1 | loop fusion | flops 4194304 | bytes 8650881 | tf_op jit(solution)/shard_map/while/body/eval_jaxpr/add | solution.py:39
  80.5 5.1 %select_add_fusion.2 = f32[16,256,256]{2,1,0:T(8,128)} fusion(f32[16,256,256]{2,1,0:T(8,128)} %get-tuple-element.195, f32[256,256]{1,0:T(8,128)S(1)} %maximum_convert_fusion.3, f32[16]{0:T(128)S(1)} %get-tuple-element.186, f32[16]{0:T(128)S(1)} %get-tuple-element.187, pred[]{:T(512)S(6)} %compare.3), kind=kLoop, calls=%fused_computation.1.clone.1 | loop fusion | flops 4194304 | bytes 8650881 | tf_op jit(solution)/shard_map/while/body/eval_jaxpr/add | solution.py:39
  100.2 7.0 %fusion.15 = f32[512,3,512]{0,2,1:T(8,128)S(1)} fusion(f32[518,3,512]{0,2,1:T(8,128)S(1)} %maximum_convert_fusion.1, f32[3,512]{1,0:T(4,128)S(1)} %copy-done.7, f32[3,512]{1,0:T(4,128)S(1)} %copy-done.8, f32[3,512]{1,0:T(4,128)S(1)} %copy-done.9, f32[3,512]{1,0:T(4,128)S(1)} %copy-done.10, f32[3,512]{1,0:T(4,128)S(1)} %copy-done.11, ...), kind=kLoop, calls=%fused_computation.21 | loop fusion | flops 10223616 | bytes 25208832 | tf_op jit(solution)/shard_map/add | solution.py:79
  108.2 11.0 %all-to-all-start = ((bf16[32,16,512]{2,1,0:T(8,128)(2,1)}), bf16[32,16,512]{2,1,0:T(8,128)(2,1)}, u32[]{:S(2)}, u32[]{:S(2)}) async-start(bf16[32,16,512]{2,1,0:T(8,128)(2,1)} %bitcast.108), calls=%async_computation | async-start | bytes 1048576 | tf_op jit(solution)/shard_map/all_to_all | solution.py:84
  120.3 13.4 %all-to-all-done = bf16[32,16,512]{2,1,0:T(8,128)(2,1)} async-done(((bf16[32,16,512]{2,1,0:T(8,128)(2,1)}), bf16[32,16,512]{2,1,0:T(8,128)(2,1)}, u32[]{:S(2)}, u32[]{:S(2)}) %all-to-all-start) | async-done | bytes 524320 | tf_op jit(solution)/shard_map/all_to_all | solution.py:84
  139.5 14.1 %fusion.5 = f32[16,16,1,64]{3,2,1,0:T(1,128)S(1)} fusion(f32[16,16,64,1]{2,3,1,0:T(1,128)S(1)} %bitcast.113, f32[64,64]{1,0:T(8,128)S(1)} %multiply_convert_fusion, f32[16,16]{1,0:T(8,128)S(1)} %copy.30, pred[64,64]{1,0:T(8,128)(4,1)S(1)} %fusion.90), kind=kOutput, calls=%fused_computation.10 | convolution fusion | flops 14680064 | bytes 152576 | tf_op jit(solution)/shard_map/cnkb,cnb->cnk/dot_general | solution.py:62
  161.5 21.4 %all_to_all.31 = bf16[16,32,512]{2,0,1:T(8,128)(2,1)S(1)} all-to-all(bf16[16,32,512]{2,0,1:T(8,128)(2,1)S(1)} %copy.33), channel_id=1, replica_groups=mesh['ctx'=32,'tp'=8] {'ctx'}, dimensions={1} | all-to-all | bytes 1048576 | tf_op jit(solution)/shard_map/all_to_all | solution.py:92
  186.2 5.8 %all-to-all-start.2 = ((bf16[8,512,512]{1,2,0:T(8,128)(2,1)}), bf16[8,512,512]{1,2,0:T(8,128)(2,1)}, u32[]{:S(2)}, u32[]{:S(2)}) async-start(bf16[8,512,512]{1,2,0:T(8,128)(2,1)} %stack.2), calls=%async_computation.2 | async-start | bytes 8388608 | tf_op jit(solution)/shard_map/all_to_all | solution.py:19
  193.2 48.8 %all-to-all-done.2 = bf16[8,512,512]{1,2,0:T(8,128)(2,1)} async-done(((bf16[8,512,512]{1,2,0:T(8,128)(2,1)}), bf16[8,512,512]{1,2,0:T(8,128)(2,1)}, u32[]{:S(2)}, u32[]{:S(2)}) %all-to-all-start.2) | async-done | bytes 4194336 | tf_op jit(solution)/shard_map/all_to_all | solution.py:19
  249.3 7.5 %convolution_convert_fusion = bf16[512,768]{1,0:T(8,128)(2,1)S(1)} fusion(bf16[512,4096]{0,1:T(8,128)(2,1)} %bitcast.107, bf16[4096,768]{0,1:T(8,128)(2,1)} %bitcast.117), kind=kOutput, calls=%fused_computation.51 | convolution fusion | flops 3221618688 | bytes 11272192 | tf_op jit(solution)/shard_map/dot_general | solution.py:101
  261.6 10.8 %collective-permute-done.1 = bf16[512,512]{1,0:T(8,128)(2,1)} collective-permute-done((bf16[512,512]{1,0:T(8,128)(2,1)S(1)}, bf16[512,512]{1,0:T(8,128)(2,1)}, u32[]{:S(2)}, u32[]{:S(2)}) %collective-permute-start.1) | collective-permute-done | bytes 524320 | tf_op jit(solution)/shard_map/ppermute | solution.py:26
  276.3 16.8 %collective-permute-done.2 = bf16[512,512]{1,0:T(8,128)(2,1)} collective-permute-done((bf16[512,512]{1,0:T(8,128)(2,1)}, bf16[512,512]{1,0:T(8,128)(2,1)}, u32[]{:S(2)}, u32[]{:S(2)}) %collective-permute-start.2) | collective-permute-done | bytes 524320 | tf_op jit(solution)/shard_map/ppermute | solution.py:26
  (125 shorter events, 70.6 us)
Async XLA Ops:
  7.2 242.1 %all-gather.2.cloned.1.call-start = ((), (), s32[]{:S(2)}) async-start(), calls=%async_computation.3 | async-start | bytes 6488064 | tf_op jit(solution)/shard_map/all_gather | solution.py:99
  8.9 90.3 %collective-permute-start = (bf16[6,3,512]{0,2,1:T(8,128)(2,1)}, bf16[6,3,512]{0,2,1:T(8,128)(2,1)S(1)}, u32[]{:S(2)}, u32[]{:S(2)}) collective-permute-start(bf16[6,3,512]{0,2,1:T(8,128)(2,1)} %copy.27), channel_id=1, source_target_pairs={{0,8},{8,16},{16,24},{24,32},{32,40},{40,48},{48,56},{56,64},{64,7... | collective-permute-start | bytes 55304 | tf_op jit(solution)/shard_map/ppermute | solution.py:26
  15.2 82.6 %copy-start.5 = (bf16[512,3,512]{2,0,1:T(8,128)(2,1)S(1)}, bf16[512,3,512]{2,0,1:T(8,128)(2,1)}, u32[]{:S(2)}) copy-start(bf16[512,3,512]{2,0,1:T(8,128)(2,1)} %param.9) | copy-start | bytes 4718596
  98.5 1.7 copy-start.7
  98.5 1.7 copy-start.8
  98.5 1.7 copy-start.9
  98.5 1.7 copy-start.10
  98.5 1.7 copy-start.11
  98.5 1.7 copy-start.12
  108.2 25.5 %all-to-all-start = ((bf16[32,16,512]{2,1,0:T(8,128)(2,1)}), bf16[32,16,512]{2,1,0:T(8,128)(2,1)}, u32[]{:S(2)}, u32[]{:S(2)}) async-start(bf16[32,16,512]{2,1,0:T(8,128)(2,1)} %bitcast.108), calls=%async_computation | async-start | bytes 1048576 | tf_op jit(solution)/shard_map/all_to_all | solution.py:84
  139.4 15.4 %copy-start = (f32[16,256,256]{2,1,0:T(8,128)S(1)}, f32[16,256,256]{2,1,0:T(8,128)}, u32[]{:S(2)}) copy-start(f32[16,256,256]{2,1,0:T(8,128)} %get-tuple-element.96) | copy-start | bytes 12582916
  139.5 15.4 %copy-start.1 = (bf16[16,64,256]{2,1,0:T(8,128)(2,1)S(1)}, bf16[16,64,256]{2,1,0:T(8,128)(2,1)}, u32[]{:S(2)}) copy-start(bf16[16,64,256]{2,1,0:T(8,128)(2,1)} %reshape.189) | copy-start | bytes 1572868
  183.0 0.8 copy-start.2
  186.2 5.8 %copy-start.13 = (f32[4096]{0:T(1024)S(1)}, f32[4096]{0:T(1024)}, u32[]{:S(2)}) copy-start(f32[4096]{0:T(1024)} %param.14) | copy-start | bytes 49156
  186.2 5.9 %copy-start.3 = (bf16[512,512]{0,1:T(8,128)(2,1)S(1)}, bf16[512,512]{0,1:T(8,128)(2,1)}, u32[]{:S(2)}) copy-start(bf16[512,512]{0,1:T(8,128)(2,1)} %copy-done.2) | copy-start | bytes 1572868
  186.2 55.7 %all-to-all-start.2 = ((bf16[8,512,512]{1,2,0:T(8,128)(2,1)}), bf16[8,512,512]{1,2,0:T(8,128)(2,1)}, u32[]{:S(2)}, u32[]{:S(2)}) async-start(bf16[8,512,512]{1,2,0:T(8,128)(2,1)} %stack.2), calls=%async_computation.2 | async-start | bytes 8388608 | tf_op jit(solution)/shard_map/all_to_all | solution.py:19
  256.9 15.6 %collective-permute-start.1 = (bf16[512,512]{1,0:T(8,128)(2,1)S(1)}, bf16[512,512]{1,0:T(8,128)(2,1)}, u32[]{:S(2)}, u32[]{:S(2)}) collective-permute-start(bf16[512,512]{1,0:T(8,128)(2,1)S(1)} %slice.119), channel_id=1, source_target_pairs={{0,8},{8,16},{16,24},{24,32},{32,40},{40,48},{48,56},{56,64},{64,7... | collective-permute-start | bytes 1572872 | tf_op jit(solution)/shard_map/ppermute | solution.py:26
  272.4 20.6 %collective-permute-start.2 = (bf16[512,512]{1,0:T(8,128)(2,1)}, bf16[512,512]{1,0:T(8,128)(2,1)}, u32[]{:S(2)}, u32[]{:S(2)}) collective-permute-start(bf16[512,512]{1,0:T(8,128)(2,1)} %collective-permute-done.1), channel_id=1, source_target_pairs={{0,8},{8,16},{16,24},{24,32},{32,40},{40,48},{48,56},{56,64},{64,7... | collective-permute-start | bytes 1572872 | tf_op jit(solution)/shard_map/ppermute | solution.py:26
  295.0 3.0 copy-start.4
  299.4 1.0 copy-start.6
Sparse Core Ops, SparseCore 0:
  12.7 73.2 all-gather.1
